TPU v7x, 32 devices: a whole 2x2x4 slice. The times are simulated.
32 devices in a mesh: grp: 2 (over y), seq: 8 (over z, x), mdl: 2 (over core).
Axes of the slice: x: 2, y: 2, z: 4, core: 2. Of those that a mesh axis runs over, the one named last changes fastest.
Arguments:
- signal: bfloat16 [2048, 2048], P(('grp', 'seq'), 'mdl'), parts along dimension 0, may hold values from -6 to 6
- gate_first: bfloat16 [2048, 2048], P(('grp', 'seq'), 'mdl'), parts along dimension 0, may hold values from -6 to 6
- gate_second: bfloat16 [2048, 2048], P(('grp', 'seq'), 'mdl'), parts along dimension 0, may hold values from -6 to 6
- spectrum_first: bfloat16 [2, 16, 128, 2048], P(None, 'seq', None, 'mdl'), may hold values from -8 to 8
- spectrum_second: bfloat16 [2, 16, 128, 2048], P(None, 'seq', None, 'mdl'), may hold values from -8 to 8
- skip_first: float32 [2048], P('mdl'), may hold values from 0.5 to 1.5
- skip_second: float32 [2048], P('mdl'), may hold values from 0.5 to 1.5
- out_weight: bfloat16 [2048, 2048], P('seq', 'mdl'), may hold values from -0.125 to 0.125
Outputs:
- block_out: bfloat16 [2048, 2048], P(('grp', 'seq'), 'mdl'), parts along dimension 0
There are 2 independent parts, one for each index of `grp`. A program takes and returns all parts, laid end to end along the dimension named above; an argument that names none is the same for every part. Nothing has to cross between parts.
All inputs are finite; a program needn't handle non-finite values.
Results may differ from a plain program's by a relative error of at most 0.0057.
Values may be sent and summed in bfloat16 or wider, within the bound.
A program may use at most 64 MiB of HBM per device.

v0:
```python
import math
import jax
import jax.numpy as jnp
from jax import lax
from jax.sharding import PartitionSpec as P


def angle_grid(first, second, modulus):
    product = first[:, None] * second[None, :] % modulus
    angles = product.astype(jnp.float32) * (2.0 * math.pi / modulus)
    return (jnp.cos(angles), jnp.sin(angles))


def mixing(form, left, right):
    return jnp.einsum(form, left, right, precision=lax.Precision.HIGHEST)


def complex_mix(form, real_table, imag_table, values_re, values_im):
    first_term = mixing(form, real_table, values_re + values_im)
    second_term = mixing(form, real_table + imag_table, values_im)
    third_term = mixing(form, imag_table - real_table, values_re)
    return (first_term - second_term, first_term + third_term)


def channel_filter(field, spectrum):
    coarse = spectrum.shape[1]
    span = spectrum.shape[2]
    count = coarse // 2
    cols = field.shape[1]
    length = coarse * span
    pencil = field.reshape(count, span, cols)
    coarse_ids = jnp.arange(coarse, dtype=jnp.int32)
    cos_a, sin_a = angle_grid(coarse_ids, jnp.arange(count, dtype=jnp.int32), coarse)
    part_re = mixing("ka,amc->kmc", cos_a, pencil)
    part_im = -mixing("ka,amc->kmc", sin_a, pencil)
    fine_ids = jnp.arange(span, dtype=jnp.int32)
    cos_t, sin_t = angle_grid(coarse_ids, fine_ids, length)
    cos_t = cos_t[:, :, None]
    sin_t = sin_t[:, :, None]
    turned_re = part_re * cos_t + part_im * sin_t
    turned_im = part_im * cos_t - part_re * sin_t
    cos_s, sin_s = angle_grid(fine_ids, fine_ids, span)
    full_re, full_im = complex_mix("qm,kmc->kqc", cos_s, -sin_s, turned_re, turned_im)
    filt_re = spectrum[0].astype(jnp.float32)
    filt_im = spectrum[1].astype(jnp.float32)
    prod_re = filt_re * full_re - filt_im * full_im
    prod_im = filt_re * full_im + filt_im * full_re
    inner_re, inner_im = complex_mix("mq,kqc->kmc", cos_s, sin_s, prod_re, prod_im)
    back_re = inner_re * cos_t - inner_im * sin_t
    back_im = inner_im * cos_t + inner_re * sin_t
    result = mixing("ka,kmc->amc", cos_a, back_re) - mixing("ka,kmc->amc", sin_a, back_im)
    return (result / length).reshape(count * span, cols)


def shards(
    signal,
    gate_first,
    gate_second,
    spectrum_first,
    spectrum_second,
    skip_first,
    skip_second,
    out_weight,
):
    seq_index = lax.axis_index("seq")
    width = signal.shape[1]
    parts_seq = lax.axis_size("seq")
    cols = width // parts_seq
    col_sig, col_first, col_second = (
        lax.all_to_all(signal, "seq", split_axis=1, concat_axis=0, tiled=True),
        lax.all_to_all(gate_first, "seq", split_axis=1, concat_axis=0, tiled=True),
        lax.all_to_all(gate_second, "seq", split_axis=1, concat_axis=0, tiled=True),
    )
    spec_one, spec_two = (
        lax.all_to_all(spectrum_first, "seq", split_axis=3, concat_axis=1, tiled=True),
        lax.all_to_all(spectrum_second, "seq", split_axis=3, concat_axis=1, tiled=True),
    )
    skip_one = lax.dynamic_slice_in_dim(skip_first, seq_index * cols, cols, 0)
    skip_two = lax.dynamic_slice_in_dim(skip_second, seq_index * cols, cols, 0)
    values = col_sig.astype(jnp.float32)
    first_conv = channel_filter(values, spec_one) + skip_one * values
    first_out = (col_first.astype(jnp.float32) * first_conv).astype(jnp.bfloat16)
    first_vals = first_out.astype(jnp.float32)
    second_conv = channel_filter(first_vals, spec_two) + skip_two * first_vals
    mixed_cols = (col_second.astype(jnp.float32) * second_conv).astype(jnp.bfloat16)
    mixed = lax.all_to_all(mixed_cols, "seq", split_axis=0, concat_axis=1, tiled=True)
    features = lax.all_gather(mixed, "mdl", axis=1, tiled=True)
    total = jnp.dot(
        features,
        lax.all_gather(out_weight, "seq", axis=0, tiled=True),
        preferred_element_type=jnp.float32,
    )
    return total.astype(jnp.bfloat16)


def solution(mesh):
    placed = (
        P(("grp", "seq"), "mdl"),
        P(("grp", "seq"), "mdl"),
        P(("grp", "seq"), "mdl"),
        P(None, "seq", None, "mdl"),
        P(None, "seq", None, "mdl"),
        P("mdl"),
        P("mdl"),
        P("seq", "mdl"),
    )
    return jax.shard_map(
        shards, mesh=mesh, in_specs=placed, out_specs=P(("grp", "seq"), "mdl"), check_vma=False
    )
```

profile of v0, /device:TPU:0, one launch (start us, length us, event | category | flops | bytes accessed | tf_op | source)
XLA Modules:
  0.0 189.6 jit_solution(12314016013267601482)
XLA Ops:
  8.6 7.4 %all-to-all-start.4 = ((bf16[128,8,128]{2,0,1:T(8,128)(2,1)}), bf16[128,8,128]{2,0,1:T(8,128)(2,1)S(1)}, u32[]{:S(2)}, u32[]{:S(2)}) async-start(bf16[128,8,128]{2,0,1:T(8,128)(2,1)} %copy.81), calls=%async_computation.4 | async-start | bytes 524288 | tf_op jit(solution)/shard_map/all_to_all | solution.py:70
  16.0 3.7 %copy.78 = bf16[2,2,128,1024]{2,1,0,3:T(2,128)(2,1)} copy(bf16[2,2,128,1024]{3,2,1,0:T(8,128)(2,1)} %param.11) | data formatting | bytes 2097152 | tf_op args[3]
  19.7 5.2 %all-to-all-done.4 = bf16[128,8,128]{2,0,1:T(8,128)(2,1)S(1)} async-done(((bf16[128,8,128]{2,0,1:T(8,128)(2,1)}), bf16[128,8,128]{2,0,1:T(8,128)(2,1)S(1)}, u32[]{:S(2)}, u32[]{:S(2)}) %all-to-all-start.4) | async-done | bytes 262176 | tf_op jit(solution)/shard_map/all_to_all | solution.py:70
  24.9 3.6 %all-to-all-start.3 = ((bf16[2,2,128,1024]{2,1,0,3:T(2,128)(2,1)}), bf16[2,2,128,1024]{2,1,0,3:T(2,128)(2,1)S(1)}, u32[]{:S(2)}, u32[]{:S(2)}) async-start(bf16[2,2,128,1024]{2,1,0,3:T(2,128)(2,1)} %copy.78), calls=%async_computation.3 | async-start | bytes 2097152 | tf_op jit(solution)/shard_map/all_to_all | solution.py:75
  30.6 2.0 %copy.73 = bf16[2,2,128,1024]{2,1,0,3:T(2,128)(2,1)} copy(bf16[2,2,128,1024]{3,2,1,0:T(8,128)(2,1)S(1)} %copy-done.1) | data formatting | bytes 2097152 | tf_op args[4]
  37.0 2.6 %fusion.179 = (f32[16,128,128]{2,0,1:T(8,128)S(1)}, f32[16,128,128]{2,0,1:T(8,128)S(1)}, f32[16,128,128]{2,0,1:T(8,128)}) fusion(f32[16,128]{0,1:T(8,128)S(1)} %copy.84, f32[16,128,128]{2,0,1:T(8,128)S(1)} %convolution_negate_fusion.1, f32[16,128]{0,1:T(8,128)S(1)} %copy.83, bf16[128,8,128]{2,0,1:T(8,128)(2,1)S(1)} %all-to-all-done.4), kind=kOutput, calls=%fused_computation.205 | convolution fusion | flops 27002624 | bytes 4472832 | tf_op jit(solution)/shard_map/ka,amc->kmc/dot_general | solution.py:15
  39.6 29.2 %all-to-all-done.3 = bf16[2,2,128,1024]{2,1,0,3:T(2,128)(2,1)S(1)} async-done(((bf16[2,2,128,1024]{2,1,0,3:T(2,128)(2,1)}), bf16[2,2,128,1024]{2,1,0,3:T(2,128)(2,1)S(1)}, u32[]{:S(2)}, u32[]{:S(2)}) %all-to-all-start.3) | async-done | bytes 1048608 | tf_op jit(solution)/shard_map/all_to_all | solution.py:75
  68.8 4.4 %all-to-all-start.1 = ((bf16[2,2,128,1024]{2,1,0,3:T(2,128)(2,1)}), bf16[2,2,128,1024]{2,1,0,3:T(2,128)(2,1)}, u32[]{:S(2)}, u32[]{:S(2)}) async-start(bf16[2,2,128,1024]{2,1,0,3:T(2,128)(2,1)} %copy.73), calls=%async_computation.1 | async-start | bytes 2097152 | tf_op jit(solution)/shard_map/all_to_all | solution.py:76
  73.3 2.1 %fusion.22 = f32[16,128,128]{2,1,0:T(8,128)S(1)} fusion(f32[16,128,128]{2,0,1:T(8,128)S(1)} %get-tuple-element.8), kind=kOutput, calls=%fused_computation.43 | convolution fusion | flops 402882560 | bytes 2097152 | tf_op jit(solution)/shard_map/qm,kmc->kqc/dot_general | solution.py:15
  75.4 2.2 %fusion.3 = f32[16,128,128]{1,2,0:T(8,128)S(1)} fusion(f32[16,128,128]{2,1,0:T(8,128)S(1)} %fusion.22, f32[16,128,128]{2,0,1:T(8,128)S(1)} %get-tuple-element.9), kind=kOutput, calls=%fused_computation.12 | convolution fusion | flops 403177472 | bytes 3145728 | tf_op jit(solution)/shard_map/qm,kmc->kqc/dot_general | solution.py:15
  77.9 2.4 %fusion.13 = (f32[16,128,128]{1,2,0:T(8,128)S(1)}, f32[16,128,128]{1,2,0:T(8,128)S(1)}) fusion(f32[16,128,128]{1,2,0:T(8,128)S(1)} %fusion.3, bf16[1,8,2,128,128]{3,4,2,1,0:T(8,128)(2,1)S(1)} %get-tuple-element.22, bf16[1,8,2,128,128]{3,4,2,1,0:T(8,128)(2,1)S(1)} %get-tuple-element.21, f32[16,128,128]{2,1,0:T(8,128)S(1)} %fusion.22, ...), kind=kOutput, calls=%fused_computation.34 | convolution fusion | flops 405274624 | bytes 6291456 | tf_op jit(solution)/shard_map/qm,kmc->kqc/dot_general | solution.py:15
  82.8 40.1 %all-to-all-done.1 = bf16[2,2,128,1024]{2,1,0,3:T(2,128)(2,1)} async-done(((bf16[2,2,128,1024]{2,1,0,3:T(2,128)(2,1)}), bf16[2,2,128,1024]{2,1,0,3:T(2,128)(2,1)}, u32[]{:S(2)}, u32[]{:S(2)}) %all-to-all-start.1) | async-done | bytes 1048608 | tf_op jit(solution)/shard_map/all_to_all | solution.py:76
  122.9 4.3 %all-to-all-start.2 = ((bf16[128,8,128]{2,0,1:T(8,128)(2,1)}), bf16[128,8,128]{2,0,1:T(8,128)(2,1)}, u32[]{:S(2)}, u32[]{:S(2)}) async-start(bf16[128,8,128]{2,0,1:T(8,128)(2,1)} %copy.76), calls=%async_computation.2 | async-start | bytes 524288 | tf_op jit(solution)/shard_map/all_to_all | solution.py:71
  127.2 2.8 %add_bitcast_fusion.1 = (f32[16,128,128]{1,2,0:T(8,128)}, f32[16,128,128]{1,2,0:T(8,128)}) fusion(f32[16,128,128]{2,1,0:T(8,128)S(1)} %convolution_add_fusion.2, f32[16,128]{1,0:T(8,128)S(1)} %get-tuple-element.23, f32[16,128]{1,0:T(8,128)S(1)} %get-tuple-element.24, f32[16,128,128]{2,1,0:T(8,128)S(1)} %fusion.26, f32[16,128,128]{1,2,0:T(8,128)S(1)} %get-tuple-element.13), kind=kOutput, calls=%fused_computation.53 | convolution fusion | flops 404733952 | bytes 5259264 | tf_op jit(solution)/shard_map/mq,kqc->kmc/dot_general | solution.py:15
  130.0 2.6 %copy.88 = f32[16,128,128]{2,0,1:T(8,128)} copy(f32[16,128,128]{1,2,0:T(8,128)} %get-tuple-element.18) | data formatting | bytes 2097152 | tf_op jit(solution)/shard_map/sub | solution.py:49
  135.8 1.9 fusion.80
  137.7 5.7 %all-to-all-start = ((bf16[128,8,128]{2,0,1:T(8,128)(2,1)}), bf16[128,8,128]{2,0,1:T(8,128)(2,1)S(1)}, u32[]{:S(2)}, u32[]{:S(2)}) async-start(bf16[128,8,128]{2,0,1:T(8,128)(2,1)} %copy.71), calls=%async_computation | async-start | bytes 524288 | tf_op jit(solution)/shard_map/all_to_all | solution.py:72
  143.4 1.9 fusion.11
  147.1 2.1 %fusion.18 = f32[16,128,128]{2,1,0:T(8,128)S(1)} fusion(f32[16,128,128]{2,0,1:T(8,128)S(1)} %get-tuple-element.5), kind=kOutput, calls=%fused_computation.39 | convolution fusion | flops 402882560 | bytes 2097152 | tf_op jit(solution)/shard_map/qm,kmc->kqc/dot_general | solution.py:15
  149.2 2.2 %fusion.1 = f32[16,128,128]{1,2,0:T(8,128)S(1)} fusion(f32[16,128,128]{2,1,0:T(8,128)S(1)} %fusion.18, f32[16,128,128]{2,0,1:T(8,128)S(1)} %get-tuple-element.6), kind=kOutput, calls=%fused_computation.5 | convolution fusion | flops 403177472 | bytes 3145728 | tf_op jit(solution)/shard_map/qm,kmc->kqc/dot_general | solution.py:15
  151.4 2.4 %fusion.15 = (f32[16,128,128]{1,2,0:T(8,128)S(1)}, f32[16,128,128]{1,2,0:T(8,128)S(1)}) fusion(f32[16,128,128]{1,2,0:T(8,128)S(1)} %fusion.1, bf16[1,8,2,128,128]{3,4,2,1,0:T(8,128)(2,1)S(1)} %get-tuple-element.20, bf16[1,8,2,128,128]{3,4,2,1,0:T(8,128)(2,1)S(1)} %get-tuple-element.19, f32[16,128,128]{2,1,0:T(8,128)S(1)} %fusion.18, ...), kind=kOutput, calls=%fused_computation.36 | convolution fusion | flops 405274624 | bytes 6291456 | tf_op jit(solution)/shard_map/qm,kmc->kqc/dot_general | solution.py:15
  162.7 14.0 %all_to_all.88 = bf16[8,128,128]{2,1,0:T(8,128)(2,1)S(1)} all-to-all(bf16[8,128,128]{2,1,0:T(8,128)(2,1)S(1)} %copy.95), channel_id=1, replica_groups=mesh['grp'=2,'seq'=8,'mdl'=2] {'seq'}, dimensions={0} | all-to-all | bytes 524288 | tf_op jit(solution)/shard_map/all_to_all | solution.py:86
  176.9 2.2 %all_gather.6 = bf16[128,2048]{0,1:T(8,128)(2,1)S(1)} all-gather(bf16[128,1024]{0,1:T(8,128)(2,1)S(1)} %bitcast.132), channel_id=1, replica_groups=mesh['grp'=2,'seq'=8,'mdl'=2] {'mdl'}, dimensions={1}, use_global_device_ids=true | all-gather | bytes 786432 | tf_op jit(solution)/shard_map/all_gather | solution.py:87
  179.1 3.6 %convolution_convert_fusion = bf16[128,1024]{1,0:T(8,128)(2,1)} fusion(bf16[128,2048]{0,1:T(8,128)(2,1)S(1)} %all_gather.6, bf16[2048,1024]{1,0:T(8,128)(2,1)} %all-gather.2.cloned.1.call-done), kind=kOutput, calls=%fused_computation.32 | convolution fusion | flops 537001984 | bytes 4980736 | tf_op jit(solution)/shard_map/dot_general | solution.py:88
  (45 shorter events, 25.3 us)
Async XLA Ops:
  6.5 23.0 %copy-start.2 = (bf16[128,1024]{1,0:T(8,128)(2,1)S(1)}, bf16[128,1024]{1,0:T(8,128)(2,1)}, u32[]{:S(2)}) copy-start(bf16[128,1024]{1,0:T(8,128)(2,1)} %param.9) | copy-start | bytes 786436
  6.5 24.0 %copy-start.1 = (bf16[2,2,128,1024]{3,2,1,0:T(8,128)(2,1)S(1)}, bf16[2,2,128,1024]{3,2,1,0:T(8,128)(2,1)}, u32[]{:S(2)}) copy-start(bf16[2,2,128,1024]{3,2,1,0:T(8,128)(2,1)} %param.12) | copy-start | bytes 3145732
  8.6 26.7 %copy-start.3 = (bf16[128,1024]{1,0:T(8,128)(2,1)S(1)}, bf16[128,1024]{1,0:T(8,128)(2,1)}, u32[]{:S(2)}) copy-start(bf16[128,1024]{1,0:T(8,128)(2,1)} %param.10) | copy-start | bytes 786436
  8.6 16.3 %all-to-all-start.4 = ((bf16[128,8,128]{2,0,1:T(8,128)(2,1)}), bf16[128,8,128]{2,0,1:T(8,128)(2,1)S(1)}, u32[]{:S(2)}, u32[]{:S(2)}) async-start(bf16[128,8,128]{2,0,1:T(8,128)(2,1)} %copy.81), calls=%async_computation.4 | async-start | bytes 524288 | tf_op jit(solution)/shard_map/all_to_all | solution.py:70
  24.9 43.9 %all-to-all-start.3 = ((bf16[2,2,128,1024]{2,1,0,3:T(2,128)(2,1)}), bf16[2,2,128,1024]{2,1,0,3:T(2,128)(2,1)S(1)}, u32[]{:S(2)}, u32[]{:S(2)}) async-start(bf16[2,2,128,1024]{2,1,0,3:T(2,128)(2,1)} %copy.78), calls=%async_computation.3 | async-start | bytes 2097152 | tf_op jit(solution)/shard_map/all_to_all | solution.py:75
  28.5 150.6 %all-gather.2.cloned.1.call-start = ((), (), s32[]{:S(2)}) async-start(), calls=%async_computation.6 | async-start | bytes 4718592 | tf_op jit(solution)/shard_map/all_gather | solution.py:90
  68.8 54.1 %all-to-all-start.1 = ((bf16[2,2,128,1024]{2,1,0,3:T(2,128)(2,1)}), bf16[2,2,128,1024]{2,1,0,3:T(2,128)(2,1)}, u32[]{:S(2)}, u32[]{:S(2)}) async-start(bf16[2,2,128,1024]{2,1,0,3:T(2,128)(2,1)} %copy.73), calls=%async_computation.1 | async-start | bytes 2097152 | tf_op jit(solution)/shard_map/all_to_all | solution.py:76
  75.4 2.5 %copy-start = (f32[16,128,128]{2,0,1:T(8,128)S(1)}, f32[16,128,128]{2,0,1:T(8,128)}, u32[]{:S(2)}) copy-start(f32[16,128,128]{2,0,1:T(8,128)} %get-tuple-element.10) | copy-start | bytes 3145732
  122.9 14.7 %all-to-all-start.2 = ((bf16[128,8,128]{2,0,1:T(8,128)(2,1)}), bf16[128,8,128]{2,0,1:T(8,128)(2,1)}, u32[]{:S(2)}, u32[]{:S(2)}) async-start(bf16[128,8,128]{2,0,1:T(8,128)(2,1)} %copy.76), calls=%async_computation.2 | async-start | bytes 524288 | tf_op jit(solution)/shard_map/all_to_all | solution.py:71
  137.7 24.2 %all-to-all-start = ((bf16[128,8,128]{2,0,1:T(8,128)(2,1)}), bf16[128,8,128]{2,0,1:T(8,128)(2,1)S(1)}, u32[]{:S(2)}, u32[]{:S(2)}) async-start(bf16[128,8,128]{2,0,1:T(8,128)(2,1)} %copy.71), calls=%async_computation | async-start | bytes 524288 | tf_op jit(solution)/shard_map/all_to_all | solution.py:72
  158.0 3.8 %copy-start.4 = (f32[128]{0:T(128)S(1)}, f32[128]{0:T(128)}, u32[]{:S(2)}) copy-start(f32[128]{0:T(128)} %dynamic_slice.7) | copy-start | bytes 1540
Sparse Core Ops, SparseCore 0:
  31.5 104.5 all-gather.1
where the time goes:
time: 191 us; the launch traced here: 190 us
  waiting for transfers between devices  75.3 us (39%)
  matrix products  37.8 us (20%)
  starting transfers between devices  25.4 us (13%)
  local copies, waits for them, and re-layouts  21.1 us (11%)
  blocking collectives  16.2 us (8%)
  between operations  13.7 us (7%)
    all_to_all x1, waiting for transfers between devices, shards(): lax.all_to_all(spectrum_second, 'seq', split_axis=3, concat_axis=1, tiled...  40.1 us
    dot_general x20, matrix products, mixing(): return jnp.einsum(form, left, right, precision=lax.Precision.HIGHEST)  34.2 us
    all_to_all x1, waiting for transfers between devices, shards(): lax.all_to_all(spectrum_first, 'seq', split_axis=3, concat_axis=1, tiled=...  29.2 us
    all_to_all x1, blocking collectives, shards(): lax.all_to_all(mixed_cols, 'seq', split_axis=0, concat_axis=1, tiled=True)  14 us
    all_to_all x1, starting transfers between devices, shards(): lax.all_to_all(signal, 'seq', split_axis=1, concat_axis=0, tiled=True)  7.38 us
    unnamed x15, local copies, waits for them, and re-layouts  7.3 us
    all_to_all x1, starting transfers between devices, shards(): lax.all_to_all(gate_second, 'seq', split_axis=1, concat_axis=0, tiled=True)  5.69 us
    all_to_all x1, waiting for transfers between devices, shards(): lax.all_to_all(signal, 'seq', split_axis=1, concat_axis=0, tiled=True)  5.23 us
  transfers between devices with their start and end apart: 6, of which 3 were waited for; matrix products, arithmetic and copies ran while one was open for 28% of the time, Pallas kernels for 0%

commit v1 on v0

--- a/solution.py
+++ b/solution.py
@@ -72,7 +72,12 @@
         lax.all_to_all(gate_second, "seq", split_axis=1, concat_axis=0, tiled=True),
     )
     spec_one, spec_two = (
-        lax.all_to_all(spectrum_first, "seq", split_axis=3, concat_axis=1, tiled=True),
+        jnp.concatenate(
+            lax.all_to_all(
+                jnp.stack(jnp.split(spectrum_first, lax.axis_size("seq"), axis=3)), "seq", 0, 0
+            ),
+            axis=1,
+        ),
         lax.all_to_all(spectrum_second, "seq", split_axis=3, concat_axis=1, tiled=True),
     )
     skip_one = lax.dynamic_slice_in_dim(skip_first, seq_index * cols, cols, 0)

time: 191 us -> 197 us (1.031)
  waiting for transfers between devices: 75.3 us -> 60.3 us
  local copies, waits for them, and re-layouts: 21.1 us -> 34.7 us
  matrix products: 37.8 us -> 40.9 us
  starting transfers between devices: 25.4 us -> 27.8 us
    all_to_all x1, waiting for transfers between devices: 40.1 us -> 30.4 us  [shards(): lax.all_to_all(spectrum_second, 'seq', split_axis=3, concat_axis=1, tiled...]
    unnamed x15 -> x19, local copies, waits for them, and re-layouts: 7.3 us -> 14.5 us
    all_to_all x1, waiting for transfers between devices: 5.23 us -> 0.01 us  [shards(): lax.all_to_all(signal, 'seq', split_axis=1, concat_axis=0, tiled=True)]
    convert_element_type x0 -> x2, local copies, waits for them, and re-layouts: none -> 5.17 us  [the longest x1 2.63 us: channel_filter(): filt_re = spectrum[0].astype(jnp.float32)]
    dot_general x20, matrix products: 34.2 us -> 37.3 us  [mixing(): return jnp.einsum(form, left, right, precision=lax.Precision.HIGHEST)]
    all_to_all x1, starting transfers between devices: 3.59 us -> 6 us  [shards(): lax.all_to_all(jnp.stack(jnp.split(spectrum_first, lax.axis_size('seq'),...]
  transfers between devices with their start and end apart: 6 -> 6, of which waited for: 3 -> 2; matrix products, arithmetic and copies ran while one was open for 28% -> 37% of each run, Pallas kernels for 0% -> 0%
where the time goes in v1:
time: 197 us; the launch traced here: 195 us
  waiting for transfers between devices  60.3 us (31%)
  matrix products  40.9 us (21%)
  local copies, waits for them, and re-layouts  34.7 us (18%)
  starting transfers between devices  27.8 us (14%)
  blocking collectives  16.2 us (8%)
  between operations  13.7 us (7%)
    dot_general x20, matrix products, mixing(): return jnp.einsum(form, left, right, precision=lax.Precision.HIGHEST)  37.3 us
    all_to_all x1, waiting for transfers between devices, shards(): lax.all_to_all(spectrum_second, 'seq', split_axis=3, concat_axis=1, tiled...  30.4 us
    all_to_all x1, waiting for transfers between devices, shards(): lax.all_to_all(jnp.stack(jnp.split(spectrum_first, lax.axis_size('seq'),...  29.2 us
    unnamed x19, local copies, waits for them, and re-layouts  14.5 us
    all_to_all x1, blocking collectives, shards(): lax.all_to_all(mixed_cols, 'seq', split_axis=0, concat_axis=1, tiled=True)  14 us
    all_to_all x1, starting transfers between devices, shards(): lax.all_to_all(signal, 'seq', split_axis=1, concat_axis=0, tiled=True)  7.38 us
    all_to_all x1, starting transfers between devices, shards(): lax.all_to_all(jnp.stack(jnp.split(spectrum_first, lax.axis_size('seq'),...  6 us
    all_to_all x1, starting transfers between devices, shards(): lax.all_to_all(gate_second, 'seq', split_axis=1, concat_axis=0, tiled=True)  5.7 us
  transfers between devices with their start and end apart: 6, of which 2 were waited for; matrix products, arithmetic and copies ran while one was open for 37% of the time, Pallas kernels for 0%

profile of v1, /device:TPU:0, one launch (start us, length us, event | category | flops | bytes accessed | tf_op | source)
XLA Modules:
  0.0 195.3 jit_solution(8802364907330384198)
XLA Ops:
  8.6 7.4 %all-to-all-start.4 = ((bf16[128,8,128]{2,0,1:T(8,128)(2,1)}), bf16[128,8,128]{2,0,1:T(8,128)(2,1)S(1)}, u32[]{:S(2)}, u32[]{:S(2)}) async-start(bf16[128,8,128]{2,0,1:T(8,128)(2,1)} %copy.81), calls=%async_computation.4 | async-start | bytes 524288 | tf_op jit(solution)/shard_map/all_to_all | solution.py:70
  28.5 6.0 %all-to-all-start.3 = ((bf16[8,2,2,128,128]{4,3,2,1,0:T(8,128)(2,1)}), bf16[8,2,2,128,128]{4,3,2,1,0:T(8,128)(2,1)S(1)}, u32[]{:S(2)}, u32[]{:S(2)}) async-start(bf16[8,2,2,128,128]{4,3,2,1,0:T(8,128)(2,1)} %bitcast_dynamic-update-slice_fusion), calls=%async_computation.3 | async-start | bytes 2097152 | tf_op jit(solution)/shard_map/all_to_all | solution.py:76
  36.6 2.0 %copy.74 = bf16[2,2,128,1024]{2,1,0,3:T(2,128)(2,1)} copy(bf16[2,2,128,1024]{3,2,1,0:T(8,128)(2,1)S(1)} %copy-done) | data formatting | bytes 2097152 | tf_op args[4]
  42.9 2.8 %fusion.179 = (f32[16,128,128]{2,0,1:T(8,128)S(1)}, f32[16,128,128]{2,0,1:T(8,128)}, f32[16,128,128]{2,0,1:T(8,128)}) fusion(f32[16,128]{0,1:T(8,128)S(1)} %copy.84, f32[16,128,128]{2,0,1:T(8,128)S(1)} %convolution_negate_fusion.1, f32[16,128]{0,1:T(8,128)S(1)} %copy.83, bf16[128,8,128]{2,0,1:T(8,128)(2,1)S(1)} %all-to-all-done.4), kind=kOutput, calls=%fused_computation.214 | convolution fusion | flops 27002624 | bytes 4472832 | tf_op jit(solution)/shard_map/ka,amc->kmc/dot_general | solution.py:15
  45.6 29.2 %all-to-all-done.3 = bf16[8,2,2,128,128]{4,3,2,1,0:T(8,128)(2,1)S(1)} async-done(((bf16[8,2,2,128,128]{4,3,2,1,0:T(8,128)(2,1)}), bf16[8,2,2,128,128]{4,3,2,1,0:T(8,128)(2,1)S(1)}, u32[]{:S(2)}, u32[]{:S(2)}) %all-to-all-start.3) | async-done | bytes 1048608 | tf_op jit(solution)/shard_map/all_to_all | solution.py:76
  74.8 4.4 %all-to-all-start.1 = ((bf16[2,2,128,1024]{2,1,0,3:T(2,128)(2,1)}), bf16[2,2,128,1024]{2,1,0,3:T(2,128)(2,1)}, u32[]{:S(2)}, u32[]{:S(2)}) async-start(bf16[2,2,128,1024]{2,1,0,3:T(2,128)(2,1)} %copy.74), calls=%async_computation.1 | async-start | bytes 2097152 | tf_op jit(solution)/shard_map/all_to_all | solution.py:81
  79.3 2.1 %fusion.22 = f32[16,128,128]{2,1,0:T(8,128)S(1)} fusion(f32[16,128,128]{2,0,1:T(8,128)S(1)} %get-tuple-element.8), kind=kOutput, calls=%fused_computation.43 | convolution fusion | flops 402882560 | bytes 2097152 | tf_op jit(solution)/shard_map/qm,kmc->kqc/dot_general | solution.py:15
  81.4 3.5 %fusion.2 = f32[16,128,128]{1,2,0:T(8,128)S(1)} fusion(f32[16,128,128]{2,1,0:T(8,128)S(1)} %fusion.22, f32[16,128,128]{2,0,1:T(8,128)} %get-tuple-element.10), kind=kOutput, calls=%fused_computation.10 | convolution fusion | flops 403177472 | bytes 3145728 | tf_op jit(solution)/shard_map/qm,kmc->kqc/dot_general | solution.py:15
  86.5 2.6 %copy.79 = f32[1,8,2,128,128]{3,4,2,1,0:T(8,128)} copy(f32[1,8,2,128,128]{4,3,2,0,1:T(8,128)} %get-tuple-element.21) | data formatting | bytes 2097152 | tf_op jit(solution)/shard_map/convert_element_type | solution.py:44
  89.2 2.5 %copy.87 = f32[1,8,2,128,128]{3,4,2,1,0:T(8,128)} copy(f32[1,8,2,128,128]{4,3,2,0,1:T(8,128)} %get-tuple-element.22) | data formatting | bytes 2097152 | tf_op jit(solution)/shard_map/convert_element_type | solution.py:45
  91.7 4.0 %fusion.15 = (f32[16,128,128]{1,2,0:T(8,128)S(1)}, f32[16,128,128]{1,2,0:T(8,128)S(1)}) fusion(f32[1,8,2,128,128]{3,4,2,1,0:T(8,128)} %copy.87, f32[16,128,128]{1,2,0:T(8,128)S(1)} %fusion.2, f32[1,8,2,128,128]{3,4,2,1,0:T(8,128)} %copy.79, f32[16,128,128]{2,1,0:T(8,128)S(1)} %fusion.22, f32[16,128,128]{2,0,1:T(8,128)} %get-tuple-element.9), kind=kOutput, calls=%fused_computation.34 | convolution fusion | flops 404750336 | bytes 7340032 | tf_op jit(solution)/shard_map/qm,kmc->kqc/dot_general | solution.py:15
  98.3 30.4 %all-to-all-done.1 = bf16[2,2,128,1024]{2,1,0,3:T(2,128)(2,1)} async-done(((bf16[2,2,128,1024]{2,1,0,3:T(2,128)(2,1)}), bf16[2,2,128,1024]{2,1,0,3:T(2,128)(2,1)}, u32[]{:S(2)}, u32[]{:S(2)}) %all-to-all-start.1) | async-done | bytes 1048608 | tf_op jit(solution)/shard_map/all_to_all | solution.py:81
  128.7 4.3 %all-to-all-start.2 = ((bf16[128,8,128]{2,0,1:T(8,128)(2,1)}), bf16[128,8,128]{2,0,1:T(8,128)(2,1)}, u32[]{:S(2)}, u32[]{:S(2)}) async-start(bf16[128,8,128]{2,0,1:T(8,128)(2,1)} %copy.77), calls=%async_computation.2 | async-start | bytes 524288 | tf_op jit(solution)/shard_map/all_to_all | solution.py:71
  133.0 2.7 %add_bitcast_fusion.1 = (f32[16,128,128]{1,2,0:T(8,128)}, f32[16,128,128]{1,2,0:T(8,128)}) fusion(f32[16,128,128]{2,1,0:T(8,128)S(1)} %convolution_add_fusion.2, f32[16,128]{1,0:T(8,128)S(1)} %get-tuple-element.23, f32[16,128]{1,0:T(8,128)S(1)} %get-tuple-element.24, f32[16,128,128]{2,1,0:T(8,128)S(1)} %fusion.26, f32[16,128,128]{1,2,0:T(8,128)S(1)} %get-tuple-element.11), kind=kOutput, calls=%fused_computation.52 | convolution fusion | flops 404733952 | bytes 5259264 | tf_op jit(solution)/shard_map/mq,kqc->kmc/dot_general | solution.py:15
  135.7 2.6 %copy.89 = f32[16,128,128]{2,0,1:T(8,128)} copy(f32[16,128,128]{1,2,0:T(8,128)} %get-tuple-element.18) | data formatting | bytes 2097152 | tf_op jit(solution)/shard_map/sub | solution.py:49
  141.5 1.9 fusion.80
  143.4 5.7 %all-to-all-start = ((bf16[128,8,128]{2,0,1:T(8,128)(2,1)}), bf16[128,8,128]{2,0,1:T(8,128)(2,1)S(1)}, u32[]{:S(2)}, u32[]{:S(2)}) async-start(bf16[128,8,128]{2,0,1:T(8,128)(2,1)} %copy.72), calls=%async_computation | async-start | bytes 524288 | tf_op jit(solution)/shard_map/all_to_all | solution.py:72
  149.1 1.9 fusion.11
  152.9 2.1 %fusion.18 = f32[16,128,128]{2,1,0:T(8,128)S(1)} fusion(f32[16,128,128]{2,0,1:T(8,128)S(1)} %get-tuple-element.5), kind=kOutput, calls=%fused_computation.39 | convolution fusion | flops 402882560 | bytes 2097152 | tf_op jit(solution)/shard_map/qm,kmc->kqc/dot_general | solution.py:15
  155.0 2.2 %fusion.1 = f32[16,128,128]{1,2,0:T(8,128)S(1)} fusion(f32[16,128,128]{2,1,0:T(8,128)S(1)} %fusion.18, f32[16,128,128]{2,0,1:T(8,128)S(1)} %get-tuple-element.6), kind=kOutput, calls=%fused_computation.5 | convolution fusion | flops 403177472 | bytes 3145728 | tf_op jit(solution)/shard_map/qm,kmc->kqc/dot_general | solution.py:15
  157.2 2.4 %fusion.13 = (f32[16,128,128]{1,2,0:T(8,128)S(1)}, f32[16,128,128]{1,2,0:T(8,128)S(1)}) fusion(f32[16,128,128]{1,2,0:T(8,128)S(1)} %fusion.1, bf16[1,8,2,128,128]{3,4,2,1,0:T(8,128)(2,1)S(1)} %get-tuple-element.20, bf16[1,8,2,128,128]{3,4,2,1,0:T(8,128)(2,1)S(1)} %get-tuple-element.19, f32[16,128,128]{2,1,0:T(8,128)S(1)} %fusion.18, ...), kind=kOutput, calls=%fused_computation.30 | convolution fusion | flops 405274624 | bytes 6291456 | tf_op jit(solution)/shard_map/qm,kmc->kqc/dot_general | solution.py:15
  168.5 14.0 %all_to_all.78 = bf16[8,128,128]{2,1,0:T(8,128)(2,1)S(1)} all-to-all(bf16[8,128,128]{2,1,0:T(8,128)(2,1)S(1)} %copy.96), channel_id=1, replica_groups=mesh['grp'=2,'seq'=8,'mdl'=2] {'seq'}, dimensions={0} | all-to-all | bytes 524288 | tf_op jit(solution)/shard_map/all_to_all | solution.py:91
  182.7 2.2 %all_gather.6 = bf16[128,2048]{0,1:T(8,128)(2,1)S(1)} all-gather(bf16[128,1024]{0,1:T(8,128)(2,1)S(1)} %bitcast.150), channel_id=1, replica_groups=mesh['grp'=2,'seq'=8,'mdl'=2] {'mdl'}, dimensions={1}, use_global_device_ids=true | all-gather | bytes 786432 | tf_op jit(solution)/shard_map/all_gather | solution.py:92
  184.8 3.6 %convolution_convert_fusion = bf16[128,1024]{1,0:T(8,128)(2,1)} fusion(bf16[128,2048]{0,1:T(8,128)(2,1)S(1)} %all_gather.6, bf16[2048,1024]{1,0:T(8,128)(2,1)} %all-gather.2.cloned.1.call-done), kind=kOutput, calls=%fused_computation.28 | convolution fusion | flops 537001984 | bytes 4980736 | tf_op jit(solution)/shard_map/dot_general | solution.py:93
  (51 shorter events, 39.1 us)
Async XLA Ops:
  6.5 29.0 %copy-start.1 = (bf16[128,1024]{1,0:T(8,128)(2,1)S(1)}, bf16[128,1024]{1,0:T(8,128)(2,1)}, u32[]{:S(2)}) copy-start(bf16[128,1024]{1,0:T(8,128)(2,1)} %param.9) | copy-start | bytes 786436
  6.5 30.0 %copy-start = (bf16[2,2,128,1024]{3,2,1,0:T(8,128)(2,1)S(1)}, bf16[2,2,128,1024]{3,2,1,0:T(8,128)(2,1)}, u32[]{:S(2)}) copy-start(bf16[2,2,128,1024]{3,2,1,0:T(8,128)(2,1)} %param.12) | copy-start | bytes 3145732
  8.6 32.5 %copy-start.2 = (bf16[128,1024]{1,0:T(8,128)(2,1)S(1)}, bf16[128,1024]{1,0:T(8,128)(2,1)}, u32[]{:S(2)}) copy-start(bf16[128,1024]{1,0:T(8,128)(2,1)} %param.10) | copy-start | bytes 786436
  8.6 19.9 %all-to-all-start.4 = ((bf16[128,8,128]{2,0,1:T(8,128)(2,1)}), bf16[128,8,128]{2,0,1:T(8,128)(2,1)S(1)}, u32[]{:S(2)}, u32[]{:S(2)}) async-start(bf16[128,8,128]{2,0,1:T(8,128)(2,1)} %copy.81), calls=%async_computation.4 | async-start | bytes 524288 | tf_op jit(solution)/shard_map/all_to_all | solution.py:70
  28.5 46.3 %all-to-all-start.3 = ((bf16[8,2,2,128,128]{4,3,2,1,0:T(8,128)(2,1)}), bf16[8,2,2,128,128]{4,3,2,1,0:T(8,128)(2,1)S(1)}, u32[]{:S(2)}, u32[]{:S(2)}) async-start(bf16[8,2,2,128,128]{4,3,2,1,0:T(8,128)(2,1)} %bitcast_dynamic-update-slice_fusion), calls=%async_computation.3 | async-start | bytes 2097152 | tf_op jit(solution)/shard_map/all_to_all | solution.py:76
  34.5 150.3 %all-gather.2.cloned.1.call-start = ((), (), s32[]{:S(2)}) async-start(), calls=%async_computation.6 | async-start | bytes 4718592 | tf_op jit(solution)/shard_map/all_gather | solution.py:95
  74.8 53.9 %all-to-all-start.1 = ((bf16[2,2,128,1024]{2,1,0,3:T(2,128)(2,1)}), bf16[2,2,128,1024]{2,1,0,3:T(2,128)(2,1)}, u32[]{:S(2)}, u32[]{:S(2)}) async-start(bf16[2,2,128,1024]{2,1,0,3:T(2,128)(2,1)} %copy.74), calls=%async_computation.1 | async-start | bytes 2097152 | tf_op jit(solution)/shard_map/all_to_all | solution.py:81
  128.7 14.7 %all-to-all-start.2 = ((bf16[128,8,128]{2,0,1:T(8,128)(2,1)}), bf16[128,8,128]{2,0,1:T(8,128)(2,1)}, u32[]{:S(2)}, u32[]{:S(2)}) async-start(bf16[128,8,128]{2,0,1:T(8,128)(2,1)} %copy.77), calls=%async_computation.2 | async-start | bytes 524288 | tf_op jit(solution)/shard_map/all_to_all | solution.py:71
  143.4 24.2 %all-to-all-start = ((bf16[128,8,128]{2,0,1:T(8,128)(2,1)}), bf16[128,8,128]{2,0,1:T(8,128)(2,1)S(1)}, u32[]{:S(2)}, u32[]{:S(2)}) async-start(bf16[128,8,128]{2,0,1:T(8,128)(2,1)} %copy.72), calls=%async_computation | async-start | bytes 524288 | tf_op jit(solution)/shard_map/all_to_all | solution.py:72
  163.8 3.8 %copy-start.3 = (f32[128]{0:T(128)S(1)}, f32[128]{0:T(128)}, u32[]{:S(2)}) copy-start(f32[128]{0:T(128)} %dynamic_slice.7) | copy-start | bytes 1540
Sparse Core Ops, SparseCore 0:
  37.5 104.3 all-gather.1
